TPU v7x, 128 devices: a whole 4x4x4 slice. The times are simulated.
128 devices in a mesh: row: 8 (over y, core), col: 16 (over x, z).
Axes of the slice: x: 4, y: 4, z: 4, core: 2. Of those that a mesh axis runs over, the one named last changes fastest.
Arguments:
- scores: float32 [32, 98304], P(None, ('row', 'col')), may hold values from -60 to 60
- tile_values: bfloat16 [8, 16, 480, 128, 128], P('row', 'col'), may hold values from 0 to 1
- tile_rows: int32 [8, 16, 480], P('row', 'col'), may hold values from 0 to 95, as said below
- tile_cols: int32 [8, 16, 480], P('row', 'col'), may hold values from 0 to 47, as said below
- tile_count: int32 [8, 16], P('row', 'col'), may hold values from 240 to 480, as said below
Outputs:
- solution: float32 [32, 98304], P(None, ('row', 'col'))
- residual: float32 [32, 98304], P(None, ('row', 'col'))
Inputs may be any that keep to these rules, and one draw needn't show every extreme that they name: `tile_rows`: on every device each local row tile is named by exactly 5 of the 480 slots. `tile_cols`: on every device each local column tile is named by exactly 10 of the slots. Only the first tile_count slots of a device are live; some device has all 480 slots live.
All inputs are finite; a program needn't handle non-finite values.
Results may differ from a plain program's by a relative error of at most 0.0031.
Values may be sent and summed in bfloat16 or wider, within the bound.
A program may use at most 128 MiB of HBM per device.

v0:
```python
import jax
import jax.numpy as jnp
from jax import lax
from jax.sharding import PartitionSpec as P

PER_ROW = 5
ITERS = 3
coupling = 0.2


def per_device(scores, tile_values, tile_rows, tile_cols, tile_count):
    tile_blocks = tile_values[0, 0]
    row_tile_ids = tile_rows[0, 0]
    col_tile_ids = tile_cols[0, 0]
    live_count = tile_count[0, 0]
    slot_count = tile_blocks.shape[0]
    tile_size = tile_blocks.shape[1]
    task_count = scores.shape[0]
    piece_len = scores.shape[1]
    row_span = piece_len * lax.axis_size("col")
    col_span = piece_len * lax.axis_size("row")
    row_tiles = row_span // tile_size
    col_tiles = col_span // tile_size
    block_slots = slot_count // PER_ROW
    live_mask = (jnp.arange(slot_count, dtype=jnp.int32) < live_count).astype(jnp.float32)
    row_weight = jnp.sum(tile_blocks, axis=2, dtype=jnp.float32) * live_mask[:, None]
    col_weight = jnp.sum(tile_blocks, axis=1, dtype=jnp.float32) * live_mask[:, None]
    row_degree_part = (
        jnp.zeros((row_tiles, tile_size), jnp.float32)
        .at[row_tile_ids]
        .add(row_weight)
        .reshape(1, row_span)
    )
    col_degree_part = (
        jnp.zeros((col_tiles, tile_size), jnp.float32)
        .at[col_tile_ids]
        .add(col_weight)
        .reshape(1, col_span)
    )

    def to_rows(partial_value):
        return lax.psum_scatter(partial_value, "col", scatter_dimension=1, tiled=True)

    def to_cols(partial_value):
        return lax.psum_scatter(partial_value, "row", scatter_dimension=1, tiled=True)

    degree = 0.5 * (to_rows(row_degree_part) + to_cols(col_degree_part))

    def inner_sums(parts):
        return lax.psum(parts, ("row", "col"))

    solution = jnp.zeros_like(scores)
    residual = scores
    direction = scores
    norm_now = inner_sums(jnp.sum(residual * residual, axis=1))
    for step_index in range(ITERS):
        graph_own_low = direction.astype(jnp.bfloat16)
        graph_col_dir = lax.all_gather(graph_own_low, "row", axis=1, tiled=True)
        graph_row_dir = lax.all_gather(graph_own_low, "col", axis=1, tiled=True)
        col_blocks = graph_col_dir.reshape(task_count, col_tiles, tile_size)
        row_blocks = graph_row_dir.reshape(task_count, row_tiles, tile_size)
        block_count = (live_count + block_slots - 1) // block_slots

        def one_block(block_index, totals):
            forward_sum, backward_sum = totals
            first_slot = block_index * block_slots
            tiles_here = lax.dynamic_slice_in_dim(tile_blocks, first_slot, block_slots, 0)
            rows_here = lax.dynamic_slice_in_dim(row_tile_ids, first_slot, block_slots, 0)
            cols_here = lax.dynamic_slice_in_dim(col_tile_ids, first_slot, block_slots, 0)
            live_here = (first_slot + jnp.arange(block_slots, dtype=jnp.int32) < live_count).astype(
                jnp.float32
            )
            col_pieces = jnp.take(col_blocks, cols_here, axis=1)
            row_pieces = jnp.take(row_blocks, rows_here, axis=1)
            forward = (
                jnp.einsum(
                    "ksd,sod->kso", col_pieces, tiles_here, preferred_element_type=jnp.float32
                )
                * live_here[None, :, None]
            )
            backward = (
                jnp.einsum(
                    "kso,sod->ksd", row_pieces, tiles_here, preferred_element_type=jnp.float32
                )
                * live_here[None, :, None]
            )
            return (
                forward_sum.at[:, rows_here, :].add(forward),
                backward_sum.at[:, cols_here, :].add(backward),
            )

        empty_sums = (
            jnp.zeros((task_count, row_tiles, tile_size), jnp.float32),
            jnp.zeros((task_count, col_tiles, tile_size), jnp.float32),
        )
        forward_sum, backward_sum = lax.fori_loop(0, block_count, one_block, empty_sums)
        forward_part = forward_sum.reshape(task_count, row_span)
        backward_part = backward_sum.reshape(task_count, col_span)
        image_field = direction + coupling * (
            degree * direction - 0.5 * (to_rows(forward_part) + to_cols(backward_part))
        )
        curvature = inner_sums(jnp.sum(direction * image_field, axis=1))
        step_size = norm_now / curvature
        solution = solution + step_size[:, None] * direction
        residual = residual - step_size[:, None] * image_field
        if step_index + 1 < ITERS:
            norm_next = inner_sums(jnp.sum(residual * residual, axis=1))
            direction = residual + (norm_next / norm_now)[:, None] * direction
            norm_now = norm_next
    return (solution, residual)


def solution(mesh):
    return jax.shard_map(
        per_device,
        mesh=mesh,
        in_specs=(
            P(None, ("row", "col")),
            P("row", "col", None, None, None),
            P("row", "col", None),
            P("row", "col", None),
            P("row", "col"),
        ),
        out_specs=(P(None, ("row", "col")), P(None, ("row", "col"))),
        check_vma=False,
    )
```

profile of v0, /device:TPU:1, one launch (start us, length us, event | category | flops | bytes accessed | tf_op | source)
XLA Modules:
  0.0 1218.0 jit_solution(540083142210740069)
XLA Ops:
  30.8 23.3 %all_gather.19 = bf16[32,12288]{1,0:T(8,128)(2,1)S(1)} all-gather(bf16[32,768]{1,0:T(8,128)(2,1)S(1)} %convert_element_type.43), channel_id=1, replica_groups=mesh['row'=8,'col'=16] {'col'}, dimensions={1}, use_global_device_ids=true | all-gather | bytes 835584 | tf_op jit(solution)/shard_map/all_gather | solution.py:59
  54.2 17.6 %all_gather.18 = bf16[32,6144]{1,0:T(8,128)(2,1)S(1)} all-gather(bf16[32,768]{1,0:T(8,128)(2,1)S(1)} %convert_element_type.43), channel_id=1, replica_groups=mesh['row'=8,'col'=16] {'row'}, dimensions={1}, use_global_device_ids=true | all-gather | bytes 442368 | tf_op jit(solution)/shard_map/all_gather | solution.py:58
  74.4 137.2 %while.36 = (s32[]{:T(128)}, f32[32,96,128]{2,0,1:T(8,128)}, f32[32,48,128]{2,0,1:T(8,128)S(1)}, s32[]{:T(128)}, s32[480]{0:T(512)}, /*index=5*/bf16[480,128,128...) while((s32[]{:T(128)}, f32[32,96,128]{2,0,1:T(8,128)}, ...), condition=%wide.region_11.14_spmd, body=%wide.region_8.13_spmd.sunk | while | flops 203689376 | bytes 23607144 | solution.py:96
  80.8 11.9 scatter_fusion
  108.4 11.8 scatter_fusion
  135.9 11.8 scatter_fusion
  190.6 11.8 scatter_fusion
  217.0 22.7 %reduce-scatter.15.cloned.1.call-done = f32[32,768]{1,0:T(8,128)} async-done(((f32[32,6144]{1,0:T(8,128)}), f32[32,768]{1,0:T(8,128)}) %reduce-scatter.15.cloned.1.call-update) | async-done | bytes 98320 | tf_op jit(solution)/shard_map/reduce_scatter | solution.py:45
  239.7 77.5 %reduce-scatter.13.cloned.1.call-done = f32[32,768]{1,0:T(8,128)} async-done(((f32[32,12288]{1,0:T(8,128)}), f32[32,768]{1,0:T(8,128)}) %reduce-scatter.13.cloned.1.call-update) | async-done | bytes 98320 | tf_op jit(solution)/shard_map/reduce_scatter | solution.py:42
  318.3 66.1 %all-reduce = (f32[32]{0:T(128)S(1)}, f32[32]{0:T(128)S(1)}) all-reduce(f32[32]{0:T(128)S(1)} %get-tuple-element.255, f32[32]{0:T(128)S(1)} %get-tuple-element.254), channel_id=1, replica_groups=mesh['row'=8,'col'=16] {'row','col'}, use_global_device_ids=true, to_apply=%region_1.0 | all-reduce | flops 64 | bytes 512 | tf_op jit(solution)/shard_map/psum | solution.py:50
  385.5 62.5 %psum.44 = f32[32]{0:T(128)S(1)} all-reduce(f32[32]{0:T(128)S(1)} %get-tuple-element.334), channel_id=1, replica_groups=mesh['row'=8,'col'=16] {'row','col'}, use_global_device_ids=true, to_apply=%region_17.20 | all-reduce | flops 32 | bytes 256 | tf_op jit(solution)/shard_map/psum | solution.py:50
  448.8 19.0 %all_gather.21 = bf16[32,12288]{1,0:T(8,128)(2,1)S(1)} all-gather(bf16[32,768]{1,0:T(8,128)(2,1)S(1)} %get-tuple-element.332), channel_id=1, replica_groups=mesh['row'=8,'col'=16] {'col'}, dimensions={1}, use_global_device_ids=true | all-gather | bytes 835584 | tf_op jit(solution)/shard_map/all_gather | solution.py:59
  467.8 18.5 %all_gather.20 = bf16[32,6144]{1,0:T(8,128)(2,1)S(1)} all-gather(bf16[32,768]{1,0:T(8,128)(2,1)S(1)} %get-tuple-element.332), channel_id=1, replica_groups=mesh['row'=8,'col'=16] {'row'}, dimensions={1}, use_global_device_ids=true | all-gather | bytes 442368 | tf_op jit(solution)/shard_map/all_gather | solution.py:58
  488.9 137.0 %while.37 = (s32[]{:T(128)}, f32[32,96,128]{2,0,1:T(8,128)}, f32[32,48,128]{2,0,1:T(8,128)S(1)}, s32[]{:T(128)}, s32[480]{0:T(512)}, /*index=5*/bf16[480,128,128...) while((s32[]{:T(128)}, f32[32,96,128]{2,0,1:T(8,128)}, ...), condition=%wide.region_21.24_spmd, body=%wide.region_18.23_spmd.sunk | while | flops 203689376 | bytes 23607556 | solution.py:96
  495.3 11.8 scatter_fusion.2
  522.6 11.8 scatter_fusion.2
  577.4 11.8 scatter_fusion.2
  604.8 11.8 scatter_fusion.2
  628.9 23.5 %reduce-scatter.19.cloned.1.call-done = f32[32,768]{1,0:T(8,128)} async-done(((f32[32,6144]{1,0:T(8,128)}), f32[32,768]{1,0:T(8,128)}) %reduce-scatter.19.cloned.1.call-update) | async-done | bytes 98320 | tf_op jit(solution)/shard_map/reduce_scatter | solution.py:45
  652.3 77.6 %reduce-scatter.17.cloned.1.call-done = f32[32,768]{1,0:T(8,128)} async-done(((f32[32,12288]{1,0:T(8,128)}), f32[32,768]{1,0:T(8,128)}) %reduce-scatter.17.cloned.1.call-update) | async-done | bytes 98320 | tf_op jit(solution)/shard_map/reduce_scatter | solution.py:42
  731.0 65.9 %psum.45 = f32[32]{0:T(128)S(1)} all-reduce(f32[32]{0:T(128)S(1)} %multiply_reduce_fusion.2), channel_id=1, replica_groups=mesh['row'=8,'col'=16] {'row','col'}, use_global_device_ids=true, to_apply=%region_25.28 | all-reduce | flops 32 | bytes 256 | tf_op jit(solution)/shard_map/psum | solution.py:50
  798.1 62.5 %psum.46 = f32[32]{0:T(128)S(1)} all-reduce(f32[32]{0:T(128)S(1)} %get-tuple-element.330), channel_id=1, replica_groups=mesh['row'=8,'col'=16] {'row','col'}, use_global_device_ids=true, to_apply=%region_27.30 | all-reduce | flops 32 | bytes 256 | tf_op jit(solution)/shard_map/psum | solution.py:50
  860.7 19.0 %all_gather.23 = bf16[32,12288]{1,0:T(8,128)(2,1)S(1)} all-gather(bf16[32,768]{1,0:T(8,128)(2,1)S(1)} %fusion.69), channel_id=1, replica_groups=mesh['row'=8,'col'=16] {'col'}, dimensions={1}, use_global_device_ids=true | all-gather | bytes 835584 | tf_op jit(solution)/shard_map/all_gather | solution.py:59
  879.7 18.8 %all_gather.22 = bf16[32,6144]{1,0:T(8,128)(2,1)S(1)} all-gather(bf16[32,768]{1,0:T(8,128)(2,1)S(1)} %fusion.69), channel_id=1, replica_groups=mesh['row'=8,'col'=16] {'row'}, dimensions={1}, use_global_device_ids=true | all-gather | bytes 442368 | tf_op jit(solution)/shard_map/all_gather | solution.py:58
  901.0 137.0 %while.38 = (s32[]{:T(128)}, f32[32,96,128]{2,0,1:T(8,128)}, f32[32,48,128]{2,0,1:T(8,128)S(1)}, s32[]{:T(128)}, s32[480]{0:T(512)}, /*index=5*/bf16[480,128,128...) while((s32[]{:T(128)}, f32[32,96,128]{2,0,1:T(8,128)}, ...), condition=%wide.region_31.34_spmd, body=%wide.region_28.33_spmd.sunk | while | flops 203689376 | bytes 23607556 | solution.py:96
  907.4 11.8 scatter_fusion.4
  934.8 11.8 scatter_fusion.4
  989.6 11.8 scatter_fusion.4
  1017.0 11.8 scatter_fusion.4
  1041.0 23.5 %reduce-scatter.23.cloned.1.call-done = f32[32,768]{1,0:T(8,128)} async-done(((f32[32,6144]{1,0:T(8,128)}), f32[32,768]{1,0:T(8,128)}) %reduce-scatter.23.cloned.1.call-update) | async-done | bytes 98320 | tf_op jit(solution)/shard_map/reduce_scatter | solution.py:45
  1064.5 77.8 %reduce-scatter.21.cloned.1.call-done = f32[32,768]{1,0:T(8,128)} async-done(((f32[32,12288]{1,0:T(8,128)}), f32[32,768]{1,0:T(8,128)}) %reduce-scatter.21.cloned.1.call-update) | async-done | bytes 98320 | tf_op jit(solution)/shard_map/reduce_scatter | solution.py:42
  1143.4 65.9 %psum.47 = f32[32]{0:T(128)S(1)} all-reduce(f32[32]{0:T(128)S(1)} %multiply_reduce_fusion), channel_id=1, replica_groups=mesh['row'=8,'col'=16] {'row','col'}, use_global_device_ids=true, to_apply=%region_35.38 | all-reduce | flops 32 | bytes 256 | tf_op jit(solution)/shard_map/psum | solution.py:50
  (263 shorter events, 318.5 us)
Async XLA Ops:
  7.2 207.5 %reduce-scatter.27.cloned.1.call-start = ((), (), s32[]{:S(2)}) async-start(), calls=%async_computation.15 | async-start | bytes 3538944
  22.9 192.9 %reduce-scatter.25.cloned.1.call-start = ((), (), s32[]{:S(2)}) async-start(), calls=%async_computation.14 | async-start | bytes 6684672
  30.0 209.8 %reduce-scatter.15.cloned.1.call-start = ((), (), s32[]{:S(2)}) async-start(), calls=%async_computation.9 | async-start | bytes 884736 | tf_op jit(solution)/shard_map/reduce_scatter | solution.py:45
  212.6 104.6 %reduce-scatter.13.cloned.1.call-start = ((), (), s32[]{:S(2)}) async-start(), calls=%async_computation.8 | async-start | bytes 1671168 | tf_op jit(solution)/shard_map/reduce_scatter | solution.py:42
  214.6 102.6 %copy-start.6 = (f32[32,768]{1,0:T(8,128)S(1)}, f32[32,768]{1,0:T(8,128)}, u32[]{:S(2)}) copy-start(f32[32,768]{1,0:T(8,128)} %param.15) | copy-start | bytes 294916
  214.6 437.7 %reduce-scatter.19.cloned.1.call-start = ((), (), s32[]{:S(2)}) async-start(), calls=%async_computation.11 | async-start | bytes 884736 | tf_op jit(solution)/shard_map/reduce_scatter | solution.py:45
  384.4 103.0 %copy-start.16 = (f32[32]{0:T(128)}, f32[32]{0:T(128)S(1)}, u32[]{:S(2)}) copy-start(f32[32]{0:T(128)S(1)} %div.22) | copy-start | bytes 388
  385.5 101.8 %copy-start.10 = (f32[32,768]{1,0:T(8,128)}, f32[32,768]{1,0:T(8,128)S(1)}, u32[]{:S(2)}) copy-start(f32[32,768]{1,0:T(8,128)S(1)} %get-tuple-element.335) | copy-start | bytes 294916
  448.0 39.3 %copy-start.20 = (f32[32]{0:T(128)}, f32[32]{0:T(128)S(1)}, u32[]{:S(2)}) copy-start(f32[32]{0:T(128)S(1)} %psum.44) | copy-start | bytes 388
  507.1 1.9 copy-start.12
  534.4 1.9 copy-start.12
  561.8 1.9 copy-start.12
  589.2 1.9 copy-start.12
  616.6 1.9 copy-start.12
  626.8 103.1 %reduce-scatter.17.cloned.1.call-start = ((), (), s32[]{:S(2)}) async-start(), calls=%async_computation.10 | async-start | bytes 1671168 | tf_op jit(solution)/shard_map/reduce_scatter | solution.py:42
  628.8 101.2 %copy-start.3 = (f32[32,768]{1,0:T(8,128)S(1)}, f32[32,768]{1,0:T(8,128)}, u32[]{:S(2)}) copy-start(f32[32,768]{1,0:T(8,128)} %get-tuple-element.333) | copy-start | bytes 294916
  628.8 168.1 %copy-start.21 = (f32[32]{0:T(128)S(1)}, f32[32]{0:T(128)}, u32[]{:S(2)}) copy-start(f32[32]{0:T(128)} %copy-done.20) | copy-start | bytes 388
  628.8 168.1 %copy-start.11 = (f32[32,768]{1,0:T(8,128)S(1)}, f32[32,768]{1,0:T(8,128)}, u32[]{:S(2)}) copy-start(f32[32,768]{1,0:T(8,128)} %copy-done.10) | copy-start | bytes 294916
  628.8 435.7 %reduce-scatter.23.cloned.1.call-start = ((), (), s32[]{:S(2)}) async-start(), calls=%async_computation.13 | async-start | bytes 884736 | tf_op jit(solution)/shard_map/reduce_scatter | solution.py:45
  796.9 102.6 %copy-start.18 = (f32[32]{0:T(128)}, f32[32]{0:T(128)S(1)}, u32[]{:S(2)}) copy-start(f32[32]{0:T(128)S(1)} %div.24) | copy-start | bytes 388
  798.1 101.5 %copy-start.8 = (f32[32,768]{1,0:T(8,128)}, f32[32,768]{1,0:T(8,128)S(1)}, u32[]{:S(2)}) copy-start(f32[32,768]{1,0:T(8,128)S(1)} %get-tuple-element.331) | copy-start | bytes 294916
  860.6 39.0 %copy-start.22 = (f32[32]{0:T(128)}, f32[32]{0:T(128)S(1)}, u32[]{:S(2)}) copy-start(f32[32]{0:T(128)S(1)} %psum.46) | copy-start | bytes 388
  860.6 39.0 %copy-start.14 = (f32[32]{0:T(128)}, f32[32]{0:T(128)S(1)}, u32[]{:S(2)}) copy-start(f32[32]{0:T(128)S(1)} %div.25) | copy-start | bytes 388
  1028.8 1.9 copy-start.13
  1039.0 103.3 %reduce-scatter.21.cloned.1.call-start = ((), (), s32[]{:S(2)}) async-start(), calls=%async_computation.12 | async-start | bytes 1671168 | tf_op jit(solution)/shard_map/reduce_scatter | solution.py:42
  1040.9 101.4 %copy-start.4 = (f32[32,768]{1,0:T(8,128)S(1)}, f32[32,768]{1,0:T(8,128)}, u32[]{:S(2)}) copy-start(f32[32,768]{1,0:T(8,128)} %get-tuple-element.333) | copy-start | bytes 294916
  1040.9 101.4 %copy-start.9 = (f32[32,768]{1,0:T(8,128)S(1)}, f32[32,768]{1,0:T(8,128)}, u32[]{:S(2)}) copy-start(f32[32,768]{1,0:T(8,128)} %copy-done.8) | copy-start | bytes 294916
  1040.9 101.4 %copy-start.15 = (f32[32]{0:T(128)S(1)}, f32[32]{0:T(128)}, u32[]{:S(2)}) copy-start(f32[32]{0:T(128)} %copy-done.14) | copy-start | bytes 388
  1040.9 168.4 %copy-start.23 = (f32[32]{0:T(128)S(1)}, f32[32]{0:T(128)}, u32[]{:S(2)}) copy-start(f32[32]{0:T(128)} %copy-done.22) | copy-start | bytes 388
  1041.0 168.4 %copy-start.7 = (f32[32,768]{1,0:T(8,128)S(1)}, f32[32,768]{1,0:T(8,128)}, u32[]{:S(2)}) copy-start(f32[32,768]{1,0:T(8,128)} %param.15) | copy-start | bytes 294916
  1041.0 168.4 %copy-start.17 = (f32[32]{0:T(128)S(1)}, f32[32]{0:T(128)}, u32[]{:S(2)}) copy-start(f32[32]{0:T(128)} %copy-done.16) | copy-start | bytes 388
  1041.0 168.4 %copy-start.19 = (f32[32]{0:T(128)S(1)}, f32[32]{0:T(128)}, u32[]{:S(2)}) copy-start(f32[32]{0:T(128)} %copy-done.18) | copy-start | bytes 388
  (8 other events, 13.4 us)
Sparse Core Ops, SparseCore 0:
  23.1 36.3 reduce-scatter.26
  62.9 82.0 reduce-scatter.24
  212.7 26.9 reduce-scatter.14
  242.8 74.3 reduce-scatter.12
  626.9 25.3 reduce-scatter.18
  655.4 74.4 reduce-scatter.16
  1039.1 25.3 reduce-scatter.22
  1067.7 74.5 reduce-scatter.20
where the time goes:
time: 1230 us; the launch traced here: 1220 us
  blocking collectives  439 us (36%)
  waiting for transfers between devices  303 us (25%)
  other arithmetic  297 us (24%)
  matrix products  98.6 us (8%)
  local copies, waits for them, and re-layouts  64 us (5%)
  between operations  15.1 us (1%)
    psum x5, blocking collectives, inner_sums(): return lax.psum(parts, ('row', 'col'))  323 us
    reduce_scatter x3, waiting for transfers between devices, to_rows(): lax.psum_scatter(partial_value, 'col', scatter_dimension=1, tiled=True)  233 us
    scatter-add x15, other arithmetic, one_block(): forward_sum.at[:, rows_here, :].add(forward)  177 us
    reduce_scatter x3, waiting for transfers between devices, to_cols(): lax.psum_scatter(partial_value, 'row', scatter_dimension=1, tiled=True)  69.7 us
    scatter-add x15, other arithmetic, one_block(): backward_sum.at[:, cols_here, :].add(backward)  66.7 us
    all_gather x3, blocking collectives, per_device(): graph_row_dir = lax.all_gather(graph_own_low, 'col', axis=1, tiled=True)  61.4 us
    dot_general x15, matrix products, one_block(): jnp.einsum('ksd,sod->kso', col_pieces, tiles_here, preferred_element_type...  55.3 us
    all_gather x3, blocking collectives, per_device(): graph_col_dir = lax.all_gather(graph_own_low, 'row', axis=1, tiled=True)  54.9 us
  transfers between devices with their start and end apart: 8, of which 6 were waited for; matrix products, arithmetic and copies ran while one was open for 13% of the time, Pallas kernels for 0%

commit v1 on v0

--- a/solution.py
+++ b/solution.py
@@ -1,3 +1,4 @@
+import functools
 import jax
 import jax.numpy as jnp
 from jax import lax
@@ -6,6 +7,14 @@
 PER_ROW = 5
 ITERS = 3
 coupling = 0.2
+
+
+def create_signs(local_array, named_axis, group_axis):
+    y1 = lax.psum(lax.psum(local_array, named_axis), group_axis)
+    return y1
+
+
+members_all_scan = functools.partial(create_signs, named_axis="row", group_axis="col")
 
 
 def per_device(scores, tile_values, tile_rows, tile_cols, tile_count):
@@ -47,7 +56,7 @@
     degree = 0.5 * (to_rows(row_degree_part) + to_cols(col_degree_part))
 
     def inner_sums(parts):
-        return lax.psum(parts, ("row", "col"))
+        return members_all_scan(parts)
 
     solution = jnp.zeros_like(scores)
     residual = scores

time: 1230 us -> 1160 us (0.943)
  blocking collectives: 439 us -> 362 us
    psum x5 -> x10, blocking collectives: 323 us -> 233 us  [create_signs(): y1 = lax.psum(lax.psum(local_array, named_axis), group_axis)]
    all_gather x3, blocking collectives: 54.9 us -> 69.4 us  [per_device(): graph_col_dir = lax.all_gather(graph_own_low, 'row', axis=1, tiled=True)]
where the time goes in v1:
time: 1160 us; the launch traced here: 1140 us
  blocking collectives  362 us (31%)
  waiting for transfers between devices  303 us (26%)
  other arithmetic  297 us (26%)
  matrix products  98.6 us (8%)
  local copies, waits for them, and re-layouts  64 us (6%)
  between operations  15.1 us (1%)
    reduce_scatter x3, waiting for transfers between devices, to_rows(): lax.psum_scatter(partial_value, 'col', scatter_dimension=1, tiled=True)  233 us
    psum x10, blocking collectives, create_signs(): y1 = lax.psum(lax.psum(local_array, named_axis), group_axis)  233 us
    scatter-add x15, other arithmetic, one_block(): forward_sum.at[:, rows_here, :].add(forward)  177 us
    reduce_scatter x3, waiting for transfers between devices, to_cols(): lax.psum_scatter(partial_value, 'row', scatter_dimension=1, tiled=True)  69.8 us
    all_gather x3, blocking collectives, per_device(): graph_col_dir = lax.all_gather(graph_own_low, 'row', axis=1, tiled=True)  69.4 us
    scatter-add x15, other arithmetic, one_block(): backward_sum.at[:, cols_here, :].add(backward)  66.7 us
    all_gather x3, blocking collectives, per_device(): graph_row_dir = lax.all_gather(graph_own_low, 'col', axis=1, tiled=True)  59.7 us
    dot_general x15, matrix products, one_block(): jnp.einsum('ksd,sod->kso', col_pieces, tiles_here, preferred_element_type...  55.3 us
  transfers between devices with their start and end apart: 8, of which 6 were waited for; matrix products, arithmetic and copies ran while one was open for 13% of the time, Pallas kernels for 0%

profile of v1, /device:TPU:1, one launch (start us, length us, event | category | flops | bytes accessed | tf_op | source)
XLA Modules:
  0.0 1140.4 jit_solution(6509980160255825990)
XLA Ops:
  30.8 23.3 %all_gather.19 = bf16[32,12288]{1,0:T(8,128)(2,1)S(1)} all-gather(bf16[32,768]{1,0:T(8,128)(2,1)S(1)} %convert_element_type.43), channel_id=1, replica_groups=mesh['row'=8,'col'=16] {'col'}, dimensions={1}, use_global_device_ids=true | all-gather | bytes 835584 | tf_op jit(solution)/shard_map/all_gather | solution.py:68
  54.2 17.6 %all_gather.18 = bf16[32,6144]{1,0:T(8,128)(2,1)S(1)} all-gather(bf16[32,768]{1,0:T(8,128)(2,1)S(1)} %convert_element_type.43), channel_id=1, replica_groups=mesh['row'=8,'col'=16] {'row'}, dimensions={1}, use_global_device_ids=true | all-gather | bytes 442368 | tf_op jit(solution)/shard_map/all_gather | solution.py:67
  74.4 137.2 %while.36 = (s32[]{:T(128)}, f32[32,96,128]{2,0,1:T(8,128)}, f32[32,48,128]{2,0,1:T(8,128)S(1)}, s32[]{:T(128)}, s32[480]{0:T(512)}, /*index=5*/bf16[480,128,128...) while((s32[]{:T(128)}, f32[32,96,128]{2,0,1:T(8,128)}, ...), condition=%wide.region_12.15_spmd, body=%wide.region_9.14_spmd.sunk | while | flops 203689376 | bytes 23607144 | solution.py:105
  80.8 11.9 %scatter_fusion = f32[32,96,128]{2,0,1:T(8,128)} fusion(f32[32,96,128]{2,0,1:T(8,128)} %get-tuple-element.571, s32[96]{0:T(128)S(1)} %get-tuple-element.524, f32[96,32,128]{2,1,0:T(8,128)S(1)} %multiply_bitcast_fusion.12), kind=kCustom, calls=%fused_computation.6.clone.1 | custom fusion | flops 393216 | bytes 4718976 | tf_op jit(solution)/shard_map/while/body/scatter-add | solution.py:97
  108.4 11.8 %scatter_fusion = f32[32,96,128]{2,0,1:T(8,128)} fusion(f32[32,96,128]{2,0,1:T(8,128)} %get-tuple-element.571, s32[96]{0:T(128)S(1)} %get-tuple-element.524, f32[96,32,128]{2,1,0:T(8,128)S(1)} %multiply_bitcast_fusion.12), kind=kCustom, calls=%fused_computation.6.clone.1 | custom fusion | flops 393216 | bytes 4718976 | tf_op jit(solution)/shard_map/while/body/scatter-add | solution.py:97
  135.9 11.8 %scatter_fusion = f32[32,96,128]{2,0,1:T(8,128)} fusion(f32[32,96,128]{2,0,1:T(8,128)} %get-tuple-element.571, s32[96]{0:T(128)S(1)} %get-tuple-element.524, f32[96,32,128]{2,1,0:T(8,128)S(1)} %multiply_bitcast_fusion.12), kind=kCustom, calls=%fused_computation.6.clone.1 | custom fusion | flops 393216 | bytes 4718976 | tf_op jit(solution)/shard_map/while/body/scatter-add | solution.py:97
  217.0 22.7 %reduce-scatter.15.cloned.1.call-done = f32[32,768]{1,0:T(8,128)} async-done(((f32[32,6144]{1,0:T(8,128)}), f32[32,768]{1,0:T(8,128)}) %reduce-scatter.15.cloned.1.call-update) | async-done | bytes 98320 | tf_op jit(solution)/shard_map/reduce_scatter | solution.py:54
  239.7 77.5 %reduce-scatter.13.cloned.1.call-done = f32[32,768]{1,0:T(8,128)} async-done(((f32[32,12288]{1,0:T(8,128)}), f32[32,768]{1,0:T(8,128)}) %reduce-scatter.13.cloned.1.call-update) | async-done | bytes 98320 | tf_op jit(solution)/shard_map/reduce_scatter | solution.py:51
  318.3 14.1 %all-reduce.1 = (f32[32]{0:T(128)S(1)}, f32[32]{0:T(128)S(1)}) all-reduce(f32[32]{0:T(128)S(1)} %get-tuple-element.255, f32[32]{0:T(128)S(1)} %get-tuple-element.254), channel_id=1, replica_groups=mesh['row'=8,'col'=16] {'row'}, use_global_device_ids=true, to_apply=%region_1.0 | all-reduce | flops 64 | bytes 512 | tf_op jit(solution)/shard_map/psum | solution.py:13
  332.4 31.1 %all-reduce = (f32[32]{0:T(128)S(1)}, f32[32]{0:T(128)S(1)}) all-reduce(f32[32]{0:T(128)S(1)} %get-tuple-element.318, f32[32]{0:T(128)S(1)} %get-tuple-element.319), channel_id=1, replica_groups=mesh['row'=8,'col'=16] {'col'}, use_global_device_ids=true, to_apply=%region_2.0 | all-reduce | flops 64 | bytes 512 | tf_op jit(solution)/shard_map/psum | solution.py:13
  364.7 19.9 %psum.88 = f32[32]{0:T(128)S(1)} all-reduce(f32[32]{0:T(128)S(1)} %get-tuple-element.336), channel_id=1, replica_groups=mesh['row'=8,'col'=16] {'row'}, use_global_device_ids=true, to_apply=%region_19.22 | all-reduce | flops 32 | bytes 256 | tf_op jit(solution)/shard_map/psum | solution.py:13
  384.6 28.5 %psum.89 = f32[32]{0:T(128)S(1)} all-reduce(f32[32]{0:T(128)S(1)} %psum.88), channel_id=1, replica_groups=mesh['row'=8,'col'=16] {'col'}, use_global_device_ids=true, to_apply=%region_20.23 | all-reduce | flops 32 | bytes 256 | tf_op jit(solution)/shard_map/psum | solution.py:13
  413.9 18.2 %all_gather.21 = bf16[32,12288]{1,0:T(8,128)(2,1)S(1)} all-gather(bf16[32,768]{1,0:T(8,128)(2,1)S(1)} %get-tuple-element.334), channel_id=1, replica_groups=mesh['row'=8,'col'=16] {'col'}, dimensions={1}, use_global_device_ids=true | all-gather | bytes 835584 | tf_op jit(solution)/shard_map/all_gather | solution.py:68
  432.1 25.9 %all_gather.20 = bf16[32,6144]{1,0:T(8,128)(2,1)S(1)} all-gather(bf16[32,768]{1,0:T(8,128)(2,1)S(1)} %get-tuple-element.334), channel_id=1, replica_groups=mesh['row'=8,'col'=16] {'row'}, dimensions={1}, use_global_device_ids=true | all-gather | bytes 442368 | tf_op jit(solution)/shard_map/all_gather | solution.py:67
  460.5 137.0 %while.37 = (s32[]{:T(128)}, f32[32,96,128]{2,0,1:T(8,128)}, f32[32,48,128]{2,0,1:T(8,128)S(1)}, s32[]{:T(128)}, s32[480]{0:T(512)}, /*index=5*/bf16[480,128,128...) while((s32[]{:T(128)}, f32[32,96,128]{2,0,1:T(8,128)}, ...), condition=%wide.region_24.27_spmd, body=%wide.region_21.26_spmd.sunk | while | flops 203689376 | bytes 23607556 | solution.py:105
  494.3 11.8 %scatter_fusion.2 = f32[32,96,128]{2,0,1:T(8,128)} fusion(f32[32,96,128]{2,0,1:T(8,128)} %get-tuple-element.613, s32[96]{0:T(128)S(1)} %get-tuple-element.538, f32[96,32,128]{2,1,0:T(8,128)S(1)} %multiply_bitcast_fusion.14), kind=kCustom, calls=%fused_computation.8.clone.1 | custom fusion | flops 393216 | bytes 4718976 | tf_op jit(solution)/shard_map/while/body/scatter-add | solution.py:97
  576.5 11.8 %scatter_fusion.2 = f32[32,96,128]{2,0,1:T(8,128)} fusion(f32[32,96,128]{2,0,1:T(8,128)} %get-tuple-element.613, s32[96]{0:T(128)S(1)} %get-tuple-element.538, f32[96,32,128]{2,1,0:T(8,128)S(1)} %multiply_bitcast_fusion.14), kind=kCustom, calls=%fused_computation.8.clone.1 | custom fusion | flops 393216 | bytes 4718976 | tf_op jit(solution)/shard_map/while/body/scatter-add | solution.py:97
  600.5 23.6 %reduce-scatter.19.cloned.1.call-done = f32[32,768]{1,0:T(8,128)} async-done(((f32[32,6144]{1,0:T(8,128)}), f32[32,768]{1,0:T(8,128)}) %reduce-scatter.19.cloned.1.call-update) | async-done | bytes 98320 | tf_op jit(solution)/shard_map/reduce_scatter | solution.py:54
  624.1 77.6 %reduce-scatter.17.cloned.1.call-done = f32[32,768]{1,0:T(8,128)} async-done(((f32[32,12288]{1,0:T(8,128)}), f32[32,768]{1,0:T(8,128)}) %reduce-scatter.17.cloned.1.call-update) | async-done | bytes 98320 | tf_op jit(solution)/shard_map/reduce_scatter | solution.py:51
  702.7 14.1 %psum.90 = f32[32]{0:T(128)S(1)} all-reduce(f32[32]{0:T(128)S(1)} %multiply_reduce_fusion.2), channel_id=1, replica_groups=mesh['row'=8,'col'=16] {'row'}, use_global_device_ids=true, to_apply=%region_28.31 | all-reduce | flops 32 | bytes 256 | tf_op jit(solution)/shard_map/psum | solution.py:13
  716.8 31.2 %psum.91 = f32[32]{0:T(128)S(1)} all-reduce(f32[32]{0:T(128)S(1)} %psum.90), channel_id=1, replica_groups=mesh['row'=8,'col'=16] {'col'}, use_global_device_ids=true, to_apply=%region_29.32 | all-reduce | flops 32 | bytes 256 | tf_op jit(solution)/shard_map/psum | solution.py:13
  749.1 19.9 %psum.92 = f32[32]{0:T(128)S(1)} all-reduce(f32[32]{0:T(128)S(1)} %get-tuple-element.332), channel_id=1, replica_groups=mesh['row'=8,'col'=16] {'row'}, use_global_device_ids=true, to_apply=%region_31.34 | all-reduce | flops 32 | bytes 256 | tf_op jit(solution)/shard_map/psum | solution.py:13
  769.1 28.5 %psum.93 = f32[32]{0:T(128)S(1)} all-reduce(f32[32]{0:T(128)S(1)} %psum.92), channel_id=1, replica_groups=mesh['row'=8,'col'=16] {'col'}, use_global_device_ids=true, to_apply=%region_32.35 | all-reduce | flops 32 | bytes 256 | tf_op jit(solution)/shard_map/psum | solution.py:13
  797.6 18.1 %all_gather.23 = bf16[32,12288]{1,0:T(8,128)(2,1)S(1)} all-gather(bf16[32,768]{1,0:T(8,128)(2,1)S(1)} %fusion.69), channel_id=1, replica_groups=mesh['row'=8,'col'=16] {'col'}, dimensions={1}, use_global_device_ids=true | all-gather | bytes 835584 | tf_op jit(solution)/shard_map/all_gather | solution.py:68
  815.7 25.9 %all_gather.22 = bf16[32,6144]{1,0:T(8,128)(2,1)S(1)} all-gather(bf16[32,768]{1,0:T(8,128)(2,1)S(1)} %fusion.69), channel_id=1, replica_groups=mesh['row'=8,'col'=16] {'row'}, dimensions={1}, use_global_device_ids=true | all-gather | bytes 442368 | tf_op jit(solution)/shard_map/all_gather | solution.py:67
  844.2 137.0 %while.38 = (s32[]{:T(128)}, f32[32,96,128]{2,0,1:T(8,128)}, f32[32,48,128]{2,0,1:T(8,128)S(1)}, s32[]{:T(128)}, s32[480]{0:T(512)}, /*index=5*/bf16[480,128,128...) while((s32[]{:T(128)}, f32[32,96,128]{2,0,1:T(8,128)}, ...), condition=%wide.region_36.39_spmd, body=%wide.region_33.38_spmd.sunk | while | flops 203689376 | bytes 23607556 | solution.py:105
  877.9 11.8 %scatter_fusion.4 = f32[32,96,128]{2,0,1:T(8,128)} fusion(f32[32,96,128]{2,0,1:T(8,128)} %get-tuple-element.655, s32[96]{0:T(128)S(1)} %get-tuple-element.552, f32[96,32,128]{2,1,0:T(8,128)S(1)} %multiply_bitcast_fusion.16), kind=kCustom, calls=%fused_computation.10.clone.1 | custom fusion | flops 393216 | bytes 4718976 | tf_op jit(solution)/shard_map/while/body/scatter-add | solution.py:97
  960.1 11.8 %scatter_fusion.4 = f32[32,96,128]{2,0,1:T(8,128)} fusion(f32[32,96,128]{2,0,1:T(8,128)} %get-tuple-element.655, s32[96]{0:T(128)S(1)} %get-tuple-element.552, f32[96,32,128]{2,1,0:T(8,128)S(1)} %multiply_bitcast_fusion.16), kind=kCustom, calls=%fused_computation.10.clone.1 | custom fusion | flops 393216 | bytes 4718976 | tf_op jit(solution)/shard_map/while/body/scatter-add | solution.py:97
  984.2 23.6 %reduce-scatter.23.cloned.1.call-done = f32[32,768]{1,0:T(8,128)} async-done(((f32[32,6144]{1,0:T(8,128)}), f32[32,768]{1,0:T(8,128)}) %reduce-scatter.23.cloned.1.call-update) | async-done | bytes 98320 | tf_op jit(solution)/shard_map/reduce_scatter | solution.py:54
  1007.7 77.7 %reduce-scatter.21.cloned.1.call-done = f32[32,768]{1,0:T(8,128)} async-done(((f32[32,12288]{1,0:T(8,128)}), f32[32,768]{1,0:T(8,128)}) %reduce-scatter.21.cloned.1.call-update) | async-done | bytes 98320 | tf_op jit(solution)/shard_map/reduce_scatter | solution.py:51
  1086.6 14.1 %psum.94 = f32[32]{0:T(128)S(1)} all-reduce(f32[32]{0:T(128)S(1)} %multiply_reduce_fusion), channel_id=1, replica_groups=mesh['row'=8,'col'=16] {'row'}, use_global_device_ids=true, to_apply=%region_40.43 | all-reduce | flops 32 | bytes 256 | tf_op jit(solution)/shard_map/psum | solution.py:13
  1100.7 31.2 %psum.95 = f32[32]{0:T(128)S(1)} all-reduce(f32[32]{0:T(128)S(1)} %psum.94), channel_id=1, replica_groups=mesh['row'=8,'col'=16] {'col'}, use_global_device_ids=true, to_apply=%region_41.44 | all-reduce | flops 32 | bytes 256 | tf_op jit(solution)/shard_map/psum | solution.py:13
  (268 shorter events, 377.4 us)
Async XLA Ops:
  7.2 207.5 %reduce-scatter.27.cloned.1.call-start = ((), (), s32[]{:S(2)}) async-start(), calls=%async_computation.15 | async-start | bytes 3538944
  22.9 192.9 %reduce-scatter.25.cloned.1.call-start = ((), (), s32[]{:S(2)}) async-start(), calls=%async_computation.14 | async-start | bytes 6684672
  30.0 209.8 %reduce-scatter.15.cloned.1.call-start = ((), (), s32[]{:S(2)}) async-start(), calls=%async_computation.9 | async-start | bytes 884736 | tf_op jit(solution)/shard_map/reduce_scatter | solution.py:54
  212.6 104.6 %reduce-scatter.13.cloned.1.call-start = ((), (), s32[]{:S(2)}) async-start(), calls=%async_computation.8 | async-start | bytes 1671168 | tf_op jit(solution)/shard_map/reduce_scatter | solution.py:51
  214.6 102.6 %copy-start.6 = (f32[32,768]{1,0:T(8,128)S(1)}, f32[32,768]{1,0:T(8,128)}, u32[]{:S(2)}) copy-start(f32[32,768]{1,0:T(8,128)} %param.15) | copy-start | bytes 294916
  214.6 409.5 %reduce-scatter.19.cloned.1.call-start = ((), (), s32[]{:S(2)}) async-start(), calls=%async_computation.11 | async-start | bytes 884736 | tf_op jit(solution)/shard_map/reduce_scatter | solution.py:54
  363.6 95.4 %copy-start.16 = (f32[32]{0:T(128)}, f32[32]{0:T(128)S(1)}, u32[]{:S(2)}) copy-start(f32[32]{0:T(128)S(1)} %div.22) | copy-start | bytes 388
  364.7 94.3 %copy-start.10 = (f32[32,768]{1,0:T(8,128)}, f32[32,768]{1,0:T(8,128)S(1)}, u32[]{:S(2)}) copy-start(f32[32,768]{1,0:T(8,128)S(1)} %get-tuple-element.337) | copy-start | bytes 294916
  413.1 45.9 %copy-start.20 = (f32[32]{0:T(128)}, f32[32]{0:T(128)S(1)}, u32[]{:S(2)}) copy-start(f32[32]{0:T(128)S(1)} %psum.89) | copy-start | bytes 388
  478.7 1.9 copy-start.12
  506.1 1.9 copy-start.12
  533.5 1.9 copy-start.12
  560.9 1.9 copy-start.12
  598.5 103.2 %reduce-scatter.17.cloned.1.call-start = ((), (), s32[]{:S(2)}) async-start(), calls=%async_computation.10 | async-start | bytes 1671168 | tf_op jit(solution)/shard_map/reduce_scatter | solution.py:51
  600.4 101.2 %copy-start.3 = (f32[32,768]{1,0:T(8,128)S(1)}, f32[32,768]{1,0:T(8,128)}, u32[]{:S(2)}) copy-start(f32[32,768]{1,0:T(8,128)} %get-tuple-element.335) | copy-start | bytes 294916
  600.5 147.5 %copy-start.21 = (f32[32]{0:T(128)S(1)}, f32[32]{0:T(128)}, u32[]{:S(2)}) copy-start(f32[32]{0:T(128)} %copy-done.20) | copy-start | bytes 388
  600.5 147.5 %copy-start.11 = (f32[32,768]{1,0:T(8,128)S(1)}, f32[32,768]{1,0:T(8,128)}, u32[]{:S(2)}) copy-start(f32[32,768]{1,0:T(8,128)} %copy-done.10) | copy-start | bytes 294916
  600.5 407.2 %reduce-scatter.23.cloned.1.call-start = ((), (), s32[]{:S(2)}) async-start(), calls=%async_computation.13 | async-start | bytes 884736 | tf_op jit(solution)/shard_map/reduce_scatter | solution.py:54
  748.0 94.6 %copy-start.18 = (f32[32]{0:T(128)}, f32[32]{0:T(128)S(1)}, u32[]{:S(2)}) copy-start(f32[32]{0:T(128)S(1)} %div.24) | copy-start | bytes 388
  749.1 93.6 %copy-start.8 = (f32[32,768]{1,0:T(8,128)}, f32[32,768]{1,0:T(8,128)S(1)}, u32[]{:S(2)}) copy-start(f32[32,768]{1,0:T(8,128)S(1)} %get-tuple-element.333) | copy-start | bytes 294916
  797.5 45.2 %copy-start.22 = (f32[32]{0:T(128)}, f32[32]{0:T(128)S(1)}, u32[]{:S(2)}) copy-start(f32[32]{0:T(128)S(1)} %psum.93) | copy-start | bytes 388
  797.5 45.2 %copy-start.14 = (f32[32]{0:T(128)}, f32[32]{0:T(128)S(1)}, u32[]{:S(2)}) copy-start(f32[32]{0:T(128)S(1)} %div.25) | copy-start | bytes 388
  862.4 1.9 copy-start.13
  944.5 1.9 copy-start.13
  982.1 103.3 %reduce-scatter.21.cloned.1.call-start = ((), (), s32[]{:S(2)}) async-start(), calls=%async_computation.12 | async-start | bytes 1671168 | tf_op jit(solution)/shard_map/reduce_scatter | solution.py:51
  984.1 101.3 %copy-start.4 = (f32[32,768]{1,0:T(8,128)S(1)}, f32[32,768]{1,0:T(8,128)}, u32[]{:S(2)}) copy-start(f32[32,768]{1,0:T(8,128)} %get-tuple-element.335) | copy-start | bytes 294916
  984.1 101.3 %copy-start.9 = (f32[32,768]{1,0:T(8,128)S(1)}, f32[32,768]{1,0:T(8,128)}, u32[]{:S(2)}) copy-start(f32[32,768]{1,0:T(8,128)} %copy-done.8) | copy-start | bytes 294916
  984.1 101.3 %copy-start.15 = (f32[32]{0:T(128)S(1)}, f32[32]{0:T(128)}, u32[]{:S(2)}) copy-start(f32[32]{0:T(128)} %copy-done.14) | copy-start | bytes 388
  984.1 147.7 %copy-start.23 = (f32[32]{0:T(128)S(1)}, f32[32]{0:T(128)}, u32[]{:S(2)}) copy-start(f32[32]{0:T(128)} %copy-done.22) | copy-start | bytes 388
  984.1 147.7 %copy-start.7 = (f32[32,768]{1,0:T(8,128)S(1)}, f32[32,768]{1,0:T(8,128)}, u32[]{:S(2)}) copy-start(f32[32,768]{1,0:T(8,128)} %param.15) | copy-start | bytes 294916
  984.1 147.7 %copy-start.17 = (f32[32]{0:T(128)S(1)}, f32[32]{0:T(128)}, u32[]{:S(2)}) copy-start(f32[32]{0:T(128)} %copy-done.16) | copy-start | bytes 388
  984.1 147.7 %copy-start.19 = (f32[32]{0:T(128)S(1)}, f32[32]{0:T(128)}, u32[]{:S(2)}) copy-start(f32[32]{0:T(128)} %copy-done.18) | copy-start | bytes 388
  (8 other events, 13.4 us)
Sparse Core Ops, SparseCore 0:
  23.1 36.3 reduce-scatter.26
  62.9 82.0 reduce-scatter.24
  212.7 26.9 reduce-scatter.14
  242.8 74.3 reduce-scatter.12
  598.6 25.4 reduce-scatter.18
  627.2 74.4 reduce-scatter.16
  982.2 25.4 reduce-scatter.22
  1010.9 74.4 reduce-scatter.20
